TPU v7x, 32 devices: a whole 2x2x4 slice. The times are simulated.
32 devices in a mesh: groups: 2 (over y), fld: 8 (over z, x), rep: 2 (over core).
Axes of the slice: x: 2, y: 2, z: 4, core: 2. Of those that a mesh axis runs over, the one named last changes fastest.
Arguments:
- feature_ids: int32 [4096, 40], P('groups', 'fld'), parts along dimension 0, may hold values from 0 to 65535, as said below
- field_slot: int32 [40], replicated, may hold values from 0 to 39, as said below
- table: bfloat16 [2621440, 64], P(('fld', 'rep')), may hold values from -48 to 48
- query_weight: bfloat16 [2, 64, 64], replicated, may hold values from -0.75 to 0.75
- key_weight: bfloat16 [2, 64, 64], replicated, may hold values from -0.75 to 0.75
- value_weight: bfloat16 [2, 64, 64], replicated, may hold values from -0.75 to 0.75
- residual_weight: bfloat16 [2, 64, 64], replicated, may hold values from -0.75 to 0.75
- out_weight: float32 [40, 64], replicated, may hold values from -0.125 to 0.125
Outputs:
- interacted: bfloat16 [40, 4096, 64], P('fld', ('groups', 'rep')), parts along dimension 1
- logits: float32 [2, 2048], P('rep', ('groups', 'fld')), parts along dimension 1
There are 2 independent parts, one for each index of `groups`. A program takes and returns all parts, laid end to end along the dimension named above; an argument that names none is the same for every part. Nothing has to cross between parts.
Inputs may be any that keep to these rules, and one draw needn't show every extreme that they name: `feature_ids`: in each column the ids lie below a table size of that slot, which differs from slot to slot. `field_slot`: distinct slots.
All inputs are finite; a program needn't handle non-finite values.
Results may differ from a plain program's by a relative error of at most 0.006.
The roundings to bfloat16 on the way count: a program that leaves them out, or rounds other values in their place, can miss the bound.
Values may be sent and summed in bfloat16 or wider, within the bound.
A program may use at most 128 MiB of HBM per device.

v0:
```python
import jax
import jax.numpy as jnp
from jax import lax
from jax.sharding import PartitionSpec as P

HEADS = 2


def from_partner(block, axis, apart):
    count = lax.axis_size(axis)
    route = []
    for low in range(count):
        high = low | 1 << apart
        if high != low and high < count:
            route += [(low, high), (high, low)]
    return lax.ppermute(block, axis, route)


def attend(layer_in, joined_weight, head_count):
    batch_rows, field_count, width = layer_in.shape
    head_size = width // head_count
    projected = jnp.einsum(
        "nfe,ed->nfd", layer_in, joined_weight, preferred_element_type=jnp.float32
    )
    query_rows = (
        projected[:, :, 0:width]
        .astype(jnp.bfloat16)
        .reshape(batch_rows, field_count, head_count, head_size)
    )
    matches = (
        projected[:, :, width : 2 * width]
        .astype(jnp.bfloat16)
        .reshape(batch_rows, field_count, head_count, head_size)
    )
    contents = (
        projected[:, :, 2 * width : 3 * width]
        .astype(jnp.bfloat16)
        .reshape(batch_rows, field_count, head_count, head_size)
    )
    skip_output = projected[:, :, 3 * width : 4 * width]
    scores = jnp.einsum(
        "nfhd,nghd->nhfg", query_rows, matches, preferred_element_type=jnp.float32
    ) / jnp.sqrt(jnp.float32(head_size))
    attention = jax.nn.softmax(scores, axis=-1).astype(jnp.bfloat16)
    mixed = jnp.einsum(
        "nhfg,nghd->nfhd", attention, contents, preferred_element_type=jnp.float32
    ).reshape(batch_rows, field_count, width)
    return jax.nn.relu(mixed + skip_output).astype(jnp.bfloat16)


def per_device(
    feature_ids,
    field_slot,
    table,
    query_weight,
    key_weight,
    value_weight,
    residual_weight,
    out_weight,
):
    total_examples, slot_per_device = feature_ids.shape
    owned_rows, width = table.shape
    fld_count = lax.axis_size("fld")
    rep_count = lax.axis_size("rep")
    rep_index = lax.axis_index("rep")
    half_batch = total_examples // rep_count
    per_peer = half_batch // fld_count
    rows_slot = owned_rows * rep_count // slot_per_device
    offsets = jnp.arange(slot_per_device, dtype=jnp.int32) * rows_slot
    slot_ids = jnp.transpose(feature_ids)
    other_half = from_partner(table, "rep", 0)
    own_ids = lax.dynamic_slice_in_dim(slot_ids, rep_index * half_batch, half_batch, 1)
    row_index = own_ids + offsets[:, None]
    owning = row_index // owned_rows
    within = row_index - owning * owned_rows
    from_own = jnp.take(table, within, axis=0)
    from_other = jnp.take(other_half, within, axis=0)
    looked = jnp.where((owning == rep_index)[:, :, None], from_own, from_other)
    slot_count = fld_count * slot_per_device
    select_mask = (field_slot[:, None] == jnp.arange(slot_count, dtype=jnp.int32)[None, :]).astype(
        jnp.bfloat16
    )
    joined = jnp.concatenate([query_weight, key_weight, value_weight, residual_weight], axis=2)
    grouped_heads = looked.reshape(slot_per_device, fld_count, per_peer // 2, 2 * width)
    arrived = lax.all_to_all(grouped_heads, "fld", split_axis=1, concat_axis=0, tiled=True)
    pair_count = arrived.shape[2]
    embedded_fields = arrived.reshape(slot_count, pair_count * 2, width)
    layer_in = jnp.einsum(
        "agb,qa->gqb", embedded_fields, select_mask, preferred_element_type=jnp.float32
    ).astype(jnp.bfloat16)
    for layer in range(joined.shape[0]):
        layer_in = attend(layer_in, joined[layer], HEADS)
    logit_rows = jnp.einsum(
        "nfd,fd->n", layer_in.astype(jnp.float32), out_weight, precision=lax.Precision.HIGHEST
    )
    placed = jnp.einsum(
        "nfd,fs->snd", layer_in, select_mask, preferred_element_type=jnp.float32
    ).astype(jnp.bfloat16)
    placed, logit_pairs = (
        placed.reshape(slot_count, 1, pair_count, 2 * width),
        logit_rows.reshape(1, 1, pair_count, 2),
    )
    returned_rows = lax.all_to_all(placed, "fld", split_axis=0, concat_axis=1, tiled=True)
    interacted = returned_rows.reshape(slot_per_device, half_batch, width)
    logits = logit_pairs.reshape(1, per_peer)
    return (interacted, logits)


def solution(mesh):
    placed = (P("groups", "fld"), P(), P(("fld", "rep"), None), P(), P(), P(), P(), P())
    return jax.shard_map(
        per_device,
        mesh=mesh,
        in_specs=placed,
        out_specs=(P("fld", ("groups", "rep"), None), P("rep", ("groups", "fld"))),
        check_vma=False,
    )
```

profile of v0, /device:TPU:0, one launch (start us, length us, event | category | flops | bytes accessed | tf_op | source)
XLA Modules:
  0.0 342.1 jit_solution(1643888605850353644)
XLA Ops:
  0.6 0.0 copy-start
  0.6 0.6 collective-permute-start
  1.2 37.2 %copy.80 = bf16[163840,64]{1,0:T(8,128)(2,1)} copy(bf16[163840,64]{0,1:T(8,128)(2,1)} %param.12) | data formatting | bytes 41943040 | tf_op args[2]
  38.4 0.1 compare_and_fusion
  38.6 53.1 %gather_fusion = bf16[5120,64]{1,0:T(8,128)(2,1)S(1)} fusion(bf16[163840,64]{1,0:T(8,128)(2,1)} %copy.80, s32[5120]{0:T(1024)S(1)} %broadcast_clamp_fusion), kind=kCustom, calls=%fused_computation.clone | custom fusion | bytes 1331200 | tf_op jit(solution)/shard_map/jit(_take)/gather | solution.py:76
  91.7 37.2 %copy.81 = bf16[163840,64]{1,0:T(8,128)(2,1)} copy(bf16[163840,64]{0,1:T(8,128)(2,1)} %collective-permute-done) | data formatting | bytes 41943040 | tf_op jit(solution)/shard_map/ppermute | solution.py:16
  128.9 76.5 %gather_fusion.1 = bf16[5120,64]{1,0:T(8,128)(2,1)} fusion(bf16[163840,64]{1,0:T(8,128)(2,1)} %copy.81, s32[5120]{0:T(1024)S(1)} %broadcast_clamp_fusion), kind=kCustom, calls=%fused_computation.1.clone | custom fusion | bytes 1331200 | tf_op jit(solution)/shard_map/jit(_take)/gather | solution.py:77
  205.4 5.0 %select_select_fusion = bf16[5,1024,64]{2,1,0:T(8,128)(2,1)S(1)} fusion(bf16[5,1024,64]{2,1,0:T(8,128)(2,1)} %bitcast.112, bf16[5,1024,64]{2,1,0:T(8,128)(2,1)S(1)} %bitcast.111, pred[5,1024]{1,0:T(8,128)(4,1)S(1)} %get-tuple-element.9, pred[5,1024]{1,0:T(8,128)(4,1)S(1)} %get-tuple-element.17), kind=kLoop, calls=%fused_computation.26 | loop fusion | flops 983040 | bytes 1976320 | tf_op jit(solution)/shard_map/jit(_where)/select_n | solution.py:78
  210.4 0.0 copy-start.3
  210.4 0.0 copy-start.4
  210.5 0.6 reshape.57
  211.1 0.9 copy.82
  212.0 6.9 %all-to-all-start = ((bf16[5,8,64,128]{3,2,0,1:T(8,128)(2,1)}), bf16[5,8,64,128]{3,2,0,1:T(8,128)(2,1)S(1)}, u32[]{:S(2)}, u32[]{:S(2)}) async-start(bf16[5,8,64,128]{3,2,0,1:T(8,128)(2,1)} %copy.82), calls=%async_computation | async-start | bytes 1310720 | tf_op jit(solution)/shard_map/all_to_all | solution.py:85
  219.0 0.1 pad_maximum_fusion
  219.1 17.7 %all-to-all-done = bf16[5,8,64,128]{3,2,0,1:T(8,128)(2,1)S(1)} async-done(((bf16[5,8,64,128]{3,2,0,1:T(8,128)(2,1)}), bf16[5,8,64,128]{3,2,0,1:T(8,128)(2,1)S(1)}, u32[]{:S(2)}, u32[]{:S(2)}) %all-to-all-start) | async-done | bytes 655392 | tf_op jit(solution)/shard_map/all_to_all | solution.py:85
  236.8 0.5 reshape.58
  237.3 1.1 copy.84
  238.4 0.4 fusion.18
  238.8 3.2 fusion.39
  241.9 2.3 fusion.38
  244.2 3.9 %copy.115 = bf16[128,40,64]{1,2,0:T(8,128)(2,1)} copy(bf16[128,40,64]{2,0,1:T(8,128)(2,1)} %get-tuple-element.15) | data formatting | bytes 1310720 | tf_op jit(solution)/shard_map/reshape | solution.py:28
  248.1 2.7 copy.116
  250.9 2.7 copy.114
  253.6 6.4 %fusion.40 = (f32[128,2,40]{2,1,0:T(2,128)S(1)}, f32[128,2,40,40]{2,3,1,0:T(8,128)}) fusion(bf16[128,40,2,32]{1,3,2,0:T(8,128)(2,1)S(1)} %bitcast.116, bf16[128,40,2,32]{1,3,2,0:T(8,128)(2,1)} %bitcast.118), kind=kOutput, calls=%fused_computation.62 | convolution fusion | flops 27443240 | bytes 2990080 | tf_op jit(solution)/shard_map/sub | solution.py:44
  260.0 6.1 %fusion.13 = f32[128,40,2,32]{1,3,2,0:T(8,128)} fusion(bf16[128,40,2,32]{1,3,2,0:T(8,128)(2,1)} %bitcast.119, f32[128,2,40,40]{2,3,1,0:T(8,128)} %get-tuple-element.21, f32[128,2,40]{2,1,0:T(2,128)S(1)} %get-tuple-element.20), kind=kOutput, calls=%fused_computation.17 | convolution fusion | flops 27033600 | bytes 3645440 | tf_op jit(solution)/shard_map/nhfg,nghd->nfhd/dot_general | solution.py:45
  266.1 5.0 %copy.93 = f32[128,40,2,32]{0,3,2,1:T(8,128)} copy(f32[128,40,2,32]{1,3,2,0:T(8,128)} %fusion.13) | data formatting | bytes 2621440 | tf_op jit(solution)/shard_map/nhfg,nghd->nfhd/transpose | solution.py:45
  271.1 2.5 slice.54
  273.6 1.8 copy.120
  275.4 2.0 fusion.17
  277.4 3.2 fusion.41
  280.5 2.3 fusion.37
  282.8 3.9 %copy.118 = bf16[128,40,64]{1,2,0:T(8,128)(2,1)} copy(bf16[128,40,64]{2,0,1:T(8,128)(2,1)} %get-tuple-element.12) | data formatting | bytes 1310720 | tf_op jit(solution)/shard_map/reshape | solution.py:28
  286.7 2.7 copy.119
  289.5 2.7 copy.117
  292.2 6.4 %fusion.42 = (f32[128,2,40]{2,1,0:T(2,128)S(1)}, f32[128,2,40,40]{2,3,1,0:T(8,128)}) fusion(bf16[128,40,2,32]{1,3,2,0:T(8,128)(2,1)S(1)} %bitcast.117, bf16[128,40,2,32]{1,3,2,0:T(8,128)(2,1)} %bitcast.120), kind=kOutput, calls=%fused_computation.64 | convolution fusion | flops 27443240 | bytes 2990080 | tf_op jit(solution)/shard_map/sub | solution.py:44
  298.6 6.1 %fusion.12 = f32[128,40,2,32]{1,3,2,0:T(8,128)} fusion(bf16[128,40,2,32]{1,3,2,0:T(8,128)(2,1)} %bitcast.121, f32[128,2,40,40]{2,3,1,0:T(8,128)} %get-tuple-element.25, f32[128,2,40]{2,1,0:T(2,128)S(1)} %get-tuple-element.24), kind=kOutput, calls=%fused_computation.16 | convolution fusion | flops 27033600 | bytes 3645440 | tf_op jit(solution)/shard_map/nhfg,nghd->nfhd/dot_general | solution.py:45
  304.7 5.0 %copy.102 = f32[128,40,2,32]{0,3,2,1:T(8,128)} copy(f32[128,40,2,32]{1,3,2,0:T(8,128)} %fusion.12) | data formatting | bytes 2621440 | tf_op jit(solution)/shard_map/nhfg,nghd->nfhd/transpose | solution.py:45
  309.7 2.5 slice.59
  312.1 1.8 copy.121
  314.0 2.0 fusion.15
  315.9 0.6 convolution_convert_fusion
  316.6 1.1 copy.105
  317.7 1.5 reshape.67
  319.2 3.7 %all-to-all-start.1 = ((bf16[40,1,64,128]{3,2,1,0:T(8,128)(2,1)}), bf16[40,1,64,128]{3,2,1,0:T(8,128)(2,1)S(1)}, u32[]{:S(2)}, u32[]{:S(2)}) async-start(bf16[40,1,64,128]{3,2,1,0:T(8,128)(2,1)} %bitcast.28), calls=%async_computation.1 | async-start | bytes 1310720 | tf_op jit(solution)/shard_map/all_to_all | solution.py:103
  322.9 0.9 convolution_bitcast_fusion
  323.8 16.5 %all-to-all-done.1 = bf16[40,1,64,128]{3,2,1,0:T(8,128)(2,1)S(1)} async-done(((bf16[40,1,64,128]{3,2,1,0:T(8,128)(2,1)}), bf16[40,1,64,128]{3,2,1,0:T(8,128)(2,1)S(1)}, u32[]{:S(2)}, u32[]{:S(2)}) %all-to-all-start.1) | async-done | bytes 655392 | tf_op jit(solution)/shard_map/all_to_all | solution.py:103
  340.3 0.5 reshape.68
  340.8 1.3 copy.108
  (20 shorter events, 0.1 us)
Async XLA Ops:
  0.6 322.2 %copy-start = (f32[40,64]{1,0:T(8,128)S(1)}, f32[40,64]{1,0:T(8,128)}, u32[]{:S(2)}) copy-start(f32[40,64]{1,0:T(8,128)} %param.17) | copy-start | bytes 30724
  0.6 91.1 %collective-permute-start = (bf16[163840,64]{0,1:T(8,128)(2,1)}, bf16[163840,64]{0,1:T(8,128)(2,1)}, u32[]{:S(2)}, u32[]{:S(2)}) collective-permute-start(bf16[163840,64]{0,1:T(8,128)(2,1)} %param.12), channel_id=1, source_target_pairs={{0,1},{1,0},{2,3},{3,2},{4,5},{5,4},{6,7},{7,6},{8,9},{9,8},{10,11... | collective-permute-start | bytes 62914568 | tf_op jit(solution)/shard_map/ppermute | solution.py:16
  1.2 37.2 %copy-start.7 = (s32[2048,5]{0,1:T(8,128)S(1)}, s32[2048,5]{0,1:T(8,128)}, u32[]{:S(2)}) copy-start(s32[2048,5]{0,1:T(8,128)} %param.10) | copy-start | bytes 122884
  210.4 8.5 %copy-start.3 = (bf16[2,64,64]{2,1,0:T(8,128)(2,1)S(1)}, bf16[2,64,64]{2,1,0:T(8,128)(2,1)}, u32[]{:S(2)}) copy-start(bf16[2,64,64]{2,1,0:T(8,128)(2,1)} %param.16) | copy-start | bytes 49156
  210.4 8.5 %copy-start.4 = (bf16[2,64,64]{2,1,0:T(8,128)(2,1)S(1)}, bf16[2,64,64]{2,1,0:T(8,128)(2,1)}, u32[]{:S(2)}) copy-start(bf16[2,64,64]{2,1,0:T(8,128)(2,1)} %param.15) | copy-start | bytes 49156
  210.4 8.5 %copy-start.5 = (bf16[2,64,64]{2,1,0:T(8,128)(2,1)S(1)}, bf16[2,64,64]{2,1,0:T(8,128)(2,1)}, u32[]{:S(2)}) copy-start(bf16[2,64,64]{2,1,0:T(8,128)(2,1)} %param.14) | copy-start | bytes 49156
  210.4 8.5 %copy-start.6 = (bf16[2,64,64]{2,1,0:T(8,128)(2,1)S(1)}, bf16[2,64,64]{2,1,0:T(8,128)(2,1)}, u32[]{:S(2)}) copy-start(bf16[2,64,64]{2,1,0:T(8,128)(2,1)} %param.13) | copy-start | bytes 49156
  212.0 24.8 %all-to-all-start = ((bf16[5,8,64,128]{3,2,0,1:T(8,128)(2,1)}), bf16[5,8,64,128]{3,2,0,1:T(8,128)(2,1)S(1)}, u32[]{:S(2)}, u32[]{:S(2)}) async-start(bf16[5,8,64,128]{3,2,0,1:T(8,128)(2,1)} %copy.82), calls=%async_computation | async-start | bytes 1310720 | tf_op jit(solution)/shard_map/all_to_all | solution.py:85
  219.0 19.4 %copy-start.8 = (s32[40]{0:T(128)S(1)}, s32[40]{0:T(128)}, u32[]{:S(2)}) copy-start(s32[40]{0:T(128)} %param.11) | copy-start | bytes 484
  250.9 2.7 copy-start.1
  289.5 2.7 copy-start.2
  319.2 21.1 %all-to-all-start.1 = ((bf16[40,1,64,128]{3,2,1,0:T(8,128)(2,1)}), bf16[40,1,64,128]{3,2,1,0:T(8,128)(2,1)S(1)}, u32[]{:S(2)}, u32[]{:S(2)}) async-start(bf16[40,1,64,128]{3,2,1,0:T(8,128)(2,1)} %bitcast.28), calls=%async_computation.1 | async-start | bytes 1310720 | tf_op jit(solution)/shard_map/all_to_all | solution.py:103
where the time goes:
time: 345 us; the launch traced here: 342 us
  local copies, waits for them, and re-layouts  253 us (73%)
  waiting for transfers between devices  34.2 us (10%)
  matrix products  33.3 us (10%)
  starting transfers between devices  11.2 us (3%)
  other arithmetic  9.19 us (3%)
    gather x1, local copies, waits for them, and re-layouts, per_device(): from_other = jnp.take(other_half, within, axis=0)  76.5 us
    gather x1, local copies, waits for them, and re-layouts, per_device(): from_own = jnp.take(table, within, axis=0)  53.1 us
    unnamed x22, local copies, waits for them, and re-layouts  42.2 us
    ppermute x1, local copies, waits for them, and re-layouts, from_partner(): return lax.ppermute(block, axis, route)  37.2 us
    all_to_all x1, waiting for transfers between devices, per_device(): lax.all_to_all(grouped_heads, 'fld', split_axis=1, concat_axis=0, tiled=T...  17.7 us
    all_to_all x1, waiting for transfers between devices, per_device(): lax.all_to_all(placed, 'fld', split_axis=0, concat_axis=1, tiled=True)  16.5 us
    sub x2, matrix products, attend(): attention = jax.nn.softmax(scores, axis=-1).astype(jnp.bfloat16)  12.7 us
    dot_general x2, matrix products, attend(): jnp.einsum('nhfg,nghd->nfhd', attention, contents, preferred_element_type...  12.2 us
  transfers between devices with their start and end apart: 3, of which 2 were waited for; matrix products, arithmetic and copies ran while one was open for 27% of the time, Pallas kernels for 0%

commit v1 on v0

v1 whole, which is shorter than its diff:
```python
import functools
import math

import jax
import jax.numpy as jnp
from jax import lax
from jax.experimental import pallas as pl
from jax.experimental.pallas import tpu as pltpu
from jax.sharding import PartitionSpec as P

HEADS = 2
f32, bf16 = jnp.float32, jnp.bfloat16

def interact_body(layers, heads, x, wt, ow, out, logit, xs, q, k, v, skip, qt, att, mt):
    fields, width, lanes = x.shape
    size = width // heads
    scale = 1.0 / math.sqrt(size)
    gb, db = 4, 4

    def layer_step(l, source):
        def project(f, carry):
            p = jnp.dot(wt[l], source[f], preferred_element_type=f32)
            base = pl.multiple_of(f * width, width)
            q[pl.ds(base, width), :] = p[0:width].astype(bf16).astype(f32)
            k[pl.ds(base, width), :] = p[width:2 * width].astype(bf16).astype(f32)
            v[pl.ds(base, width), :] = p[2 * width:3 * width].astype(bf16).astype(f32)
            skip[pl.ds(base, width), :] = p[3 * width:4 * width]
            return carry
        lax.fori_loop(0, fields, project, 0, unroll=4)

        def turn(d, carry):
            qt[pl.ds(pl.multiple_of(d * fields, 8), fields), :] = q[pl.ds(d, fields, stride=width), :] * scale
            return carry
        lax.fori_loop(0, width, turn, 0, unroll=8)

        for h in range(heads):
            def match(gi, top):
                acc = [jnp.zeros((fields, lanes), f32) for _ in range(gb)]
                for d in range(h * size, (h + 1) * size):
                    qd = qt[d * fields:(d + 1) * fields, :]
                    for j in range(gb):
                        row = k[pl.ds((gi * gb + j) * width + d, 1), :]
                        acc[j] = acc[j] + qd * row
                for j in range(gb):
                    att[h, gi * gb + j] = acc[j]
                    top = jnp.maximum(top, acc[j])
                return top
            top = lax.fori_loop(0, fields // gb, match, jnp.full((fields, lanes), -jnp.inf, f32))

            def expo(g, total):
                e = jnp.exp(att[h, g] - top)
                att[h, g] = e
                return total + e
            total = lax.fori_loop(0, fields, expo, jnp.zeros((fields, lanes), f32), unroll=4)
            inverse = 1.0 / total

            def norm(g, carry):
                att[h, g] = (att[h, g] * inverse).astype(bf16).astype(f32)
                return carry
            lax.fori_loop(0, fields, norm, 0, unroll=4)

        def mix(di, carry):
            h = di // (size // db)
            acc = [jnp.zeros((fields, lanes), f32) for _ in range(db)]
            for g in range(fields):
                a = att[h, g]
                for j in range(db):
                    row = v[pl.ds(g * width + di * db + j, 1), :]
                    acc[j] = acc[j] + a * row
            for j in range(db):
                mt[pl.ds(pl.multiple_of((di * db + j) * fields, 8), fields), :] = acc[j]
            return carry
        lax.fori_loop(0, width // db, mix, 0)

    def finish(f):
        m = mt[pl.ds(f, width, stride=fields), :]
        s = skip[pl.ds(pl.multiple_of(f * width, width), width), :]
        return jnp.maximum(m + s, 0.0).astype(bf16)

    for l in range(layers):
        layer_step(l, x if l == 0 else xs)
        if l < layers - 1:
            def close(f, carry):
                xs[f] = finish(f)
                return carry
            lax.fori_loop(0, fields, close, 0, unroll=4)
        else:
            total = jnp.zeros((width, lanes), f32)
            for f in range(fields):
                hid = finish(f)
                out[f] = hid
                total = total + hid.astype(f32) * ow[:, f:f + 1]
            logit[...] = jnp.sum(total, axis=0, keepdims=True)

def interact(x, wt, ow):
    fields, width, lanes = x.shape
    layers = wt.shape[0]
    flat = pltpu.VMEM((fields * width, lanes), f32)
    return pl.pallas_call(
        functools.partial(interact_body, layers, HEADS),
        out_shape=(jax.ShapeDtypeStruct(x.shape, bf16), jax.ShapeDtypeStruct((1, lanes), f32)),
        in_specs=[pl.BlockSpec(memory_space=pltpu.VMEM)] * 3,
        out_specs=(pl.BlockSpec(memory_space=pltpu.VMEM),) * 2,
        scratch_shapes=[pltpu.VMEM(x.shape, bf16), flat, flat, flat, flat, flat,
                        pltpu.VMEM((HEADS, fields, fields, lanes), f32), flat],
        compiler_params=pltpu.CompilerParams(vmem_limit_bytes=40 << 20),
    )(x, wt, ow)


def lookup_body(ready, rows, valid, table, out, held, sems):
    tiles, slots, width, lanes = out.shape
    piece = table.shape[1] // sems.shape[0]
    copies = [
        pltpu.make_async_copy(
            table.at[:, c * piece:(c + 1) * piece], held.at[:, c * piece:(c + 1) * piece], sems.at[c]
        )
        for c in range(sems.shape[0])
    ]
    for copy in copies:
        copy.start()
    lane = lax.broadcasted_iota(jnp.int32, (1, lanes), 1)
    done = 0
    for j in range(slots):
        while done < len(copies) and done * piece < ready[j]:
            copies[done].wait()
            done += 1

        def tile(t, carry):
            acc = jnp.zeros((width, lanes), bf16)
            for i in range(lanes):
                row = rows[j, t * lanes + i]
                start = pl.multiple_of((row >> 7) * 128, 128)
                block = pltpu.roll(held[:, pl.ds(start, lanes)], (i - row) & 127, 1)
                acc = jnp.where(lane == i, block, acc)
            keep = valid[j, pl.ds(t, 1), :] > 0
            out[t, j] = jnp.where(keep, acc, jnp.zeros_like(acc))
            return carry
        lax.fori_loop(0, tiles, tile, 0)
    for copy in copies[done:]:
        copy.wait()


def pieces(owned):
    return next(c for c in (5, 4, 3, 2, 1) if owned % (c * 128) == 0)


def lookup(rows, valid, table_t, ready):
    slots, tiles, lanes = valid.shape
    width, owned = table_t.shape
    return pl.pallas_call(
        functools.partial(lookup_body, ready),
        out_shape=jax.ShapeDtypeStruct((tiles, slots, width, lanes), bf16),
        in_specs=[
            pl.BlockSpec(memory_space=pltpu.SMEM),
            pl.BlockSpec(memory_space=pltpu.VMEM),
            pl.BlockSpec(memory_space=pl.ANY),
        ],
        out_specs=pl.BlockSpec(memory_space=pltpu.VMEM),
        scratch_shapes=[
            pltpu.VMEM((width, owned), bf16),
            pltpu.SemaphoreType.DMA((pieces(owned),)),
        ],
        compiler_params=pltpu.CompilerParams(vmem_limit_bytes=48 << 20),
    )(rows, valid, table_t)


def per_device(
    feature_ids, field_slot, table, query_weight, key_weight, value_weight, residual_weight, out_weight
):
    examples, slots = feature_ids.shape
    owned, width = table.shape
    fld = lax.axis_size("fld")
    rep = lax.axis_size("rep")
    me = lax.axis_index("rep")
    rows_slot = owned * rep // slots
    lanes = examples // rep // fld
    firsts = [r * owned // rows_slot for r in range(rep)]
    lasts = [-(-(r + 1) * owned // rows_slot) for r in range(rep)]
    near = max(b - a for a, b in zip(firsts, lasts))
    firsts = [min(a, slots - near) for a in firsts]
    ready = [
        max(min(owned, (a + j + 1) * rows_slot - r * owned) for r, a in enumerate(firsts))
        for j in range(near)
    ]
    first = sum((me == r) * a for r, a in enumerate(firsts)).astype(jnp.int32)
    near_ids = lax.dynamic_slice_in_dim(jnp.transpose(feature_ids), first, near, 0)
    offset = (first + jnp.arange(near, dtype=jnp.int32)) * rows_slot - me * owned
    rows = near_ids + offset[:, None]
    valid = ((rows >= 0) & (rows < owned)).astype(jnp.int32)
    rows = jnp.clip(rows, 0, owned - 1)
    found = lookup(rows, valid.reshape(near, -1, lanes), jnp.transpose(table), ready)
    found = found.reshape(rep, fld, near, width, lanes)
    own = lax.dynamic_index_in_dim(found, me, 0, False)
    looked = jnp.zeros((fld, slots, width, lanes), bf16)
    looked = lax.dynamic_update_slice_in_dim(looked, own, first, 1)
    for step in range(1, rep):
        route = [(r, (r + step) % rep) for r in range(rep)]
        got = lax.ppermute(lax.dynamic_index_in_dim(found, (me + step) % rep, 0, False), "rep", route)
        source = (me - step) % rep
        start = sum((source == r) * a for r, a in enumerate(firsts)).astype(jnp.int32)
        old = lax.dynamic_slice_in_dim(looked, start, near, 1)
        looked = lax.dynamic_update_slice_in_dim(looked, old + got, start, 1)
    arrived = lax.all_to_all(looked, "fld", split_axis=0, concat_axis=0, tiled=True)
    layer_in = arrived.reshape(fld * slots, width, lanes)
    joined = jnp.concatenate([query_weight, key_weight, value_weight, residual_weight], axis=2)
    weights = jnp.swapaxes(joined, 1, 2)
    fields = field_slot.shape[0]
    whole = fields == fld * slots
    if whole:
        order = field_slot[:, None] == jnp.arange(fields, dtype=jnp.int32)[None, :]
        weight_t = jnp.sum(jnp.where(order[:, None, :], out_weight[:, :, None], 0.0), axis=0)
    else:
        layer_in = jnp.take(layer_in, field_slot, axis=0)
        weight_t = jnp.transpose(out_weight)
    hidden, logits = interact(layer_in, weights, weight_t)
    if not whole:
        hidden = jnp.zeros((fld * slots, width, lanes), bf16).at[field_slot].set(hidden)
    placed = hidden.reshape(fld, slots, width, lanes)
    back = lax.all_to_all(placed, "fld", split_axis=0, concat_axis=0, tiled=True)
    interacted = jnp.transpose(back, (1, 0, 3, 2)).reshape(slots, fld * lanes, width)
    return interacted, logits


def solution(mesh):
    placed = (P("groups", "fld"), P(), P(("fld", "rep"), None), P(), P(), P(), P(), P())
    return jax.shard_map(
        per_device,
        mesh=mesh,
        in_specs=placed,
        out_specs=(P("fld", ("groups", "rep"), None), P("rep", ("groups", "fld"))),
        check_vma=False,
    )
```

time: 345 us -> 119 us (0.34)
  local copies, waits for them, and re-layouts: 253 us -> 3.27 us
  Pallas kernels: 0 us -> 64.6 us
  matrix products: 33.3 us -> 0 us
  blocking collectives: 0 us -> 21.2 us
  waiting for transfers between devices: 34.2 us -> 17 us
  other arithmetic: 9.19 us -> 4.12 us
  starting transfers between devices: 11.2 us -> 7.33 us
    gather x2 -> x0, local copies, waits for them, and re-layouts: 130 us -> none  [the longest x1 76.5 us: per_device(): from_other = jnp.take(other_half, within, axis=0)]
    pallas_call x0 -> x2, Pallas kernels: none -> 64.6 us  [the longest x1 39.1 us: lookup(): pl.pallas_call(functools.partial(lookup_body, ready), out_shape=jax.Shape...]
    unnamed x22 -> x17, local copies, waits for them, and re-layouts: 42.2 us -> 0.41 us
    ppermute x1 -> x0, local copies, waits for them, and re-layouts: 37.2 us -> none  [from_partner(): return lax.ppermute(block, axis, route)]
    reshape x12 -> x1, local copies, waits for them, and re-layouts: 23.9 us -> 0.94 us  [per_device(): jnp.transpose(back, (1, 0, 3, 2)).reshape(slots, fld * lanes, width)]
    all_to_all x0 -> x1, blocking collectives: none -> 21.2 us  [per_device(): lax.all_to_all(placed, 'fld', split_axis=0, concat_axis=0, tiled=True)]
    dot_general x7 -> x0, matrix products: 20.5 us -> none  [the longest x2 12.2 us: attend(): jnp.einsum('nhfg,nghd->nfhd', attention, contents, preferred_element_type...]
    all_to_all x2 -> x1, waiting for transfers between devices: 34.2 us -> 17 us  [per_device(): lax.all_to_all(looked, 'fld', split_axis=0, concat_axis=0, tiled=True)]
  transfers between devices with their start and end apart: 3 -> 2, of which waited for: 2 -> 1; matrix products, arithmetic and copies ran while one was open for 27% -> 2% of each run, Pallas kernels for 0% -> 0%
where the time goes in v1:
time: 119 us; the launch traced here: 118 us
  Pallas kernels  64.6 us (54%)
  blocking collectives  21.2 us (18%)
  waiting for transfers between devices  17 us (14%)
  starting transfers between devices  7.33 us (6%)
  other arithmetic  4.12 us (3%)
  local copies, waits for them, and re-layouts  3.27 us (3%)
    pallas_call x1, Pallas kernels, lookup(): pl.pallas_call(functools.partial(lookup_body, ready), out_shape=jax.Shape...  39.1 us
    pallas_call x1, Pallas kernels, interact(): pl.pallas_call(functools.partial(interact_body, layers, HEADS), out_shape...  25.5 us
    all_to_all x1, blocking collectives, per_device(): lax.all_to_all(placed, 'fld', split_axis=0, concat_axis=0, tiled=True)  21.2 us
    all_to_all x1, waiting for transfers between devices, per_device(): lax.all_to_all(looked, 'fld', split_axis=0, concat_axis=0, tiled=True)  17 us
    all_to_all x1, starting transfers between devices, per_device(): lax.all_to_all(looked, 'fld', split_axis=0, concat_axis=0, tiled=True)  6.97 us
  transfers between devices with their start and end apart: 2, of which 1 were waited for; matrix products, arithmetic and copies ran while one was open for 2% of the time, Pallas kernels for 0%

profile of v1, /device:TPU:0, one launch (start us, length us, event | category | flops | bytes accessed | tf_op | source)
XLA Modules:
  0.0 118.4 jit_solution(9450799331735906608)
XLA Ops:
  0.6 0.0 copy-start
  0.6 0.0 copy-start.1
  0.7 0.0 copy-start.2
  0.7 0.0 copy-start.3
  0.7 0.0 copy-start.5
  0.7 0.0 copy-start.4
  0.7 0.9 clamp_bitcast_fusion.rows
  1.6 0.9 convert_bitcast_fusion
  2.6 39.1 %shard_map.95 = bf16[16,3,64,128]{3,2,1,0:T(8,128)(2,1)S(1)} custom-call(s32[3,2048]{1,0:T(4,128)S(1)} %clamp_bitcast_fusion.rows, s32[3,16,128]{2,1,0:T(8,128)S(1)} %bitcast.28, bf16[64,163840]{1,0:T(8,128)(2,1)} %bitcast.29), custom_call_target="tpu_custom_call" | custom-call | tf_op jit(solution)/shard_map/pallas_call | solution.py:150
  41.7 0.4 collective-permute-start
  42.1 1.0 broadcast_in_dim.28
  43.1 0.8 bitcast_dynamic-update-slice_fusion
  43.9 0.0 collective-permute-done
  43.9 1.9 %add_dynamic-update-slice_fusion = bf16[8,5,64,128]{3,2,1,0:T(8,128)(2,1)} fusion(bf16[8,5,64,128]{3,2,1,0:T(8,128)(2,1)} %bitcast_dynamic-update-slice_fusion, s32[]{:T(128)S(6)} %mul.19, bf16[8,3,64,128]{3,2,1,0:T(8,128)(2,1)S(1)} %collective-permute-done), kind=kLoop, calls=%fused_computation.3 | loop fusion | flops 786432 | bytes 1179652 | tf_op jit(solution)/shard_map/dynamic_update_slice | solution.py:202
  45.8 7.0 %all-to-all-start = ((bf16[8,5,64,128]{3,2,1,0:T(8,128)(2,1)}), bf16[8,5,64,128]{3,2,1,0:T(8,128)(2,1)S(1)}, u32[]{:S(2)}, u32[]{:S(2)}) async-start(bf16[8,5,64,128]{3,2,1,0:T(8,128)(2,1)} %add_dynamic-update-slice_fusion), calls=%async_computation | async-start | bytes 1310720 | tf_op jit(solution)/shard_map/all_to_all | solution.py:203
  52.8 0.0 copy-done
  52.8 0.1 copy.18
  52.9 0.0 copy-done.1
  52.9 0.1 copy.17
  53.0 0.0 copy-done.2
  53.0 0.1 copy.16
  53.1 0.0 copy-done.3
  53.1 0.1 copy.15
  53.2 0.0 copy-done.5
  53.2 0.1 iota_compare_fusion
  53.3 0.0 copy-done.4
  53.3 0.3 select_reduce_fusion
  53.6 0.1 copy.19.ow
  53.7 17.0 %all-to-all-done = bf16[8,5,64,128]{3,2,1,0:T(8,128)(2,1)S(1)} async-done(((bf16[8,5,64,128]{3,2,1,0:T(8,128)(2,1)}), bf16[8,5,64,128]{3,2,1,0:T(8,128)(2,1)S(1)}, u32[]{:S(2)}, u32[]{:S(2)}) %all-to-all-start) | async-done | bytes 655392 | tf_op jit(solution)/shard_map/all_to_all | solution.py:203
  70.7 25.5 %shard_map.96 = (bf16[40,64,128]{2,1,0:T(8,128)(2,1)S(1)}, f32[1,128]{1,0:T(1,128)}) custom-call(bf16[40,64,128]{2,1,0:T(8,128)(2,1)S(1)} %bitcast.26, bf16[2,256,64]{2,1,0:T(8,128)(2,1)S(1)} %maximum_bitcast_fusion.wt, f32[64,40]{1,0:T(8,128)S(1)} %copy.19.ow), custom_call_target="tpu_custom_call" | custom-call | tf_op jit(solution)/shard_map/pallas_call | solution.py:99
  96.2 21.2 %all_to_all.10 = bf16[8,5,64,128]{3,2,1,0:T(8,128)(2,1)S(1)} all-to-all(bf16[8,5,64,128]{3,2,1,0:T(8,128)(2,1)S(1)} %bitcast.27), channel_id=1, replica_groups=mesh['groups'=2,'fld'=8,'rep'=2] {'fld'}, dimensions={0} | all-to-all | bytes 1310720 | tf_op jit(solution)/shard_map/all_to_all | solution.py:219
  117.5 0.9 copy_bitcast_fusion
  (4 shorter events, 0.1 us)
Async XLA Ops:
  0.6 52.1 %copy-start = (bf16[2,64,64]{2,1,0:T(8,128)(2,1)S(1)}, bf16[2,64,64]{2,1,0:T(8,128)(2,1)}, u32[]{:S(2)}) copy-start(bf16[2,64,64]{2,1,0:T(8,128)(2,1)} %param.14) | copy-start | bytes 49156
  0.6 52.2 %copy-start.1 = (bf16[2,64,64]{2,1,0:T(8,128)(2,1)S(1)}, bf16[2,64,64]{2,1,0:T(8,128)(2,1)}, u32[]{:S(2)}) copy-start(bf16[2,64,64]{2,1,0:T(8,128)(2,1)} %param.13) | copy-start | bytes 49156
  0.7 52.3 %copy-start.2 = (bf16[2,64,64]{2,1,0:T(8,128)(2,1)S(1)}, bf16[2,64,64]{2,1,0:T(8,128)(2,1)}, u32[]{:S(2)}) copy-start(bf16[2,64,64]{2,1,0:T(8,128)(2,1)} %param.12) | copy-start | bytes 49156
  0.7 52.4 %copy-start.3 = (bf16[2,64,64]{2,1,0:T(8,128)(2,1)S(1)}, bf16[2,64,64]{2,1,0:T(8,128)(2,1)}, u32[]{:S(2)}) copy-start(bf16[2,64,64]{2,1,0:T(8,128)(2,1)} %param.11) | copy-start | bytes 49156
  0.7 52.5 %copy-start.5 = (s32[40]{0:T(128)S(1)}, s32[40]{0:T(128)}, u32[]{:S(2)}) copy-start(s32[40]{0:T(128)} %param.9) | copy-start | bytes 484
  0.7 52.6 %copy-start.4 = (f32[40,64]{1,0:T(8,128)S(1)}, f32[40,64]{1,0:T(8,128)}, u32[]{:S(2)}) copy-start(f32[40,64]{1,0:T(8,128)} %param.15) | copy-start | bytes 30724
  41.7 2.2 %collective-permute-start = (bf16[8,3,64,128]{3,2,1,0:T(8,128)(2,1)S(1)}, bf16[8,3,64,128]{3,2,1,0:T(8,128)(2,1)S(1)}, u32[]{:S(2)}, u32[]{:S(2)}) collective-permute-start(bf16[8,3,64,128]{3,2,1,0:T(8,128)(2,1)S(1)} %dynamic-slice_bitcast_fusion), channel_id=1, source_target_pairs={{0,1},{1,0},{2,3},{3,2},{4,5},{5,4},{6,7},{7,6},{8,9},{9,8},{10,11... | collective-permute-start | bytes 1179656 | tf_op jit(solution)/shard_map/ppermute | solution.py:198
  45.8 24.9 %all-to-all-start = ((bf16[8,5,64,128]{3,2,1,0:T(8,128)(2,1)}), bf16[8,5,64,128]{3,2,1,0:T(8,128)(2,1)S(1)}, u32[]{:S(2)}, u32[]{:S(2)}) async-start(bf16[8,5,64,128]{3,2,1,0:T(8,128)(2,1)} %add_dynamic-update-slice_fusion), calls=%async_computation | async-start | bytes 1310720 | tf_op jit(solution)/shard_map/all_to_all | solution.py:203

commit v2 on v1

v2 whole, which is shorter than its diff:
```python
import functools
import math

import jax
import jax.numpy as jnp
from jax import lax
from jax.experimental import pallas as pl
from jax.experimental.pallas import tpu as pltpu
from jax.sharding import PartitionSpec as P

HEADS = 2
f32, bf16 = jnp.float32, jnp.bfloat16

MESH = pl.DeviceIdType.MESH


def greet(peers):
    barrier = pltpu.get_barrier_semaphore()
    for peer in peers:
        pl.semaphore_signal(barrier, inc=1, device_id=peer, device_id_type=MESH)
    return barrier


def interact_body(
    layers, heads, firsts, slots, fld, rep, found, wt, ow, out, logit,
    xs, q, k, v, skip, qt, att, mt, *links
):
    fields, width, lanes = xs.shape
    near = found.shape[1]
    size = width // heads
    scale = 1.0 / math.sqrt(size)
    gb, db = 4, 4
    if fld:
        staged, send, recv, keep, got, hop_send, hop_recv = links
        me = lax.axis_index("fld")
        half = lax.axis_index("rep")

        def peer(n, c):
            return lax.rem(me + n, fld), lax.rem(half + c, rep)

        def hop(n, c):
            to_fld, to_rep = peer(n, c)
            return pltpu.make_async_remote_copy(
                src_ref=found.at[to_rep * fld + to_fld], dst_ref=got.at[half * fld + me],
                send_sem=hop_send.at[n, c], recv_sem=hop_recv.at[n, c],
                device_id={"fld": to_fld, "rep": to_rep}, device_id_type=MESH,
            )
        others = [(n, c) for n in range(fld) for c in range(rep) if n or c]
        barrier = greet([{"fld": peer(n, c)[0], "rep": peer(n, c)[1]} for n, c in others])
        mine = pltpu.make_async_copy(found.at[half * fld + me], got.at[half * fld + me], keep.at[HEADS])
        mine.start()
        pl.semaphore_wait(barrier, len(others))
        for n, c in others:
            hop(n, c).start()

        def parcel(h, n):
            dest = lax.rem(me + 1 + n, fld)
            part = pl.ds(h * size, size)
            return pltpu.make_async_remote_copy(
                src_ref=staged.at[h, dest],
                dst_ref=out.at[:, part, pl.ds(pl.multiple_of(me * lanes, lanes), lanes)],
                send_sem=send.at[h, n], recv_sem=recv.at[h, n],
                device_id={"fld": dest}, device_id_type=MESH,
            )

    def project_one(l, f, value):
        p = jnp.dot(wt[l], value, preferred_element_type=f32)
        base = pl.multiple_of(f * width, width)
        q[pl.ds(base, width), :] = p[0:width].astype(bf16).astype(f32)
        k[pl.ds(base, width), :] = p[width:2 * width].astype(bf16).astype(f32)
        v[pl.ds(base, width), :] = p[2 * width:3 * width].astype(bf16).astype(f32)
        skip[pl.ds(base, width), :] = p[3 * width:4 * width]

    def turn(d, carry):
        qt[pl.ds(pl.multiple_of(d * fields, 8), fields), :] = q[pl.ds(d, fields, stride=width), :] * scale
        return carry

    def attend(h):
        def match(gi, top):
            acc = [jnp.zeros((fields, lanes), f32) for _ in range(gb)]
            for d in range(h * size, (h + 1) * size):
                qd = qt[d * fields:(d + 1) * fields, :]
                for j in range(gb):
                    row = k[pl.ds((gi * gb + j) * width + d, 1), :]
                    acc[j] = acc[j] + qd * row
            for j in range(gb):
                att[gi * gb + j] = acc[j]
                top = jnp.maximum(top, acc[j])
            return top
        top = lax.fori_loop(0, fields // gb, match, jnp.full((fields, lanes), -jnp.inf, f32))

        def expo(g, total):
            e = jnp.exp(att[g] - top)
            att[g] = e
            return total + e
        total = lax.fori_loop(0, fields, expo, jnp.zeros((fields, lanes), f32), unroll=4)
        inverse = 1.0 / total

        def norm(g, carry):
            att[g] = (att[g] * inverse).astype(bf16).astype(f32)
            return carry
        lax.fori_loop(0, fields, norm, 0, unroll=4)

        def mix(di, carry):
            acc = [jnp.zeros((fields, lanes), f32) for _ in range(db)]
            for g in range(fields):
                a = att[g]
                for j in range(db):
                    row = v[pl.ds(g * width + di * db + j, 1), :]
                    acc[j] = acc[j] + a * row
            for j in range(db):
                mt[pl.ds(pl.multiple_of((di * db + j) * fields, 8), fields), :] = acc[j]
            return carry
        lax.fori_loop(h * size // db, (h + 1) * size // db, mix, 0)

    def finish(f, h):
        m = mt[pl.ds(h * size * fields + f, size, stride=fields), :]
        s = skip[pl.ds(pl.multiple_of(f * width + h * size, size), size), :]
        return jnp.maximum(m + s, 0.0).astype(bf16)

    for l in range(layers):
        if l == 0:
            if fld:
                mine.wait()

                def arrive(n, carry):
                    p = lax.rem(me - n + fld, fld)
                    for s in range(slots):
                        terms = [got[r * fld + p, s - a] for r, a in enumerate(firsts) if 0 <= s - a < near]
                        project_one(0, p * slots + s, sum(terms[1:], terms[0]))
                    return carry

                def await_arrive(n, carry):
                    for c in range(rep):
                        hop(n, c).wait_recv()
                    return arrive(n, carry)
                for c in range(1, rep):
                    hop(0, c).wait_recv()
                arrive(0, 0)
                lax.fori_loop(1, fld, await_arrive, 0)
            else:
                def first_layer(f, carry):
                    project_one(0, f, found[f, 0])
                    return carry
                lax.fori_loop(0, fields, first_layer, 0, unroll=4)
        else:
            def next_layer(f, carry):
                project_one(l, f, xs[f])
                return carry
            lax.fori_loop(0, fields, next_layer, 0, unroll=4)
        lax.fori_loop(0, width, turn, 0, unroll=8)
        if l < layers - 1:
            for h in range(heads):
                attend(h)

            def close(f, carry):
                for h in range(heads):
                    xs[f, h * size:(h + 1) * size, :] = finish(f, h)
                return carry
            lax.fori_loop(0, fields, close, 0, unroll=4)
        else:
            total = jnp.zeros((size, lanes), f32)
            for h in range(heads):
                attend(h)
                for f in range(fields):
                    hid = finish(f, h)
                    if fld:
                        staged[h, f // slots, f % slots] = hid
                    else:
                        out[f, h * size:(h + 1) * size, :] = hid
                    total = total + hid.astype(f32) * ow[h * size:(h + 1) * size, f:f + 1]
                if fld:
                    for n in range(fld - 1):
                        parcel(h, n).start()
            logit[...] = jnp.sum(total, axis=0, keepdims=True)
    if fld:
        for h in range(heads):
            own = pltpu.make_async_copy(
                staged.at[h, me],
                out.at[:, pl.ds(h * size, size), pl.ds(pl.multiple_of(me * lanes, lanes), lanes)],
                keep.at[h],
            )
            own.start()
            own.wait()
        for h in range(heads):
            for n in range(fld - 1):
                parcel(h, n).wait()
        for n, c in others:
            hop(n, c).wait_send()


def interact(found, wt, ow, firsts, slots, fld, rep):
    fields = ow.shape[1]
    near, width, lanes = found.shape[1:]
    layers = wt.shape[0]
    flat = pltpu.VMEM((fields * width, lanes), f32)
    out_shape, links, extra = (fields, width, lanes), [], {}
    if fld:
        size = width // HEADS
        out_shape = (slots, width, fld * lanes)
        links = [
            pltpu.VMEM((HEADS, fld, slots, size, lanes), bf16),
            pltpu.SemaphoreType.DMA((HEADS, fld - 1)),
            pltpu.SemaphoreType.DMA((HEADS, fld - 1)),
            pltpu.SemaphoreType.DMA((HEADS + 1,)),
            pltpu.VMEM(found.shape, bf16),
            pltpu.SemaphoreType.DMA((fld, rep)),
            pltpu.SemaphoreType.DMA((fld, rep)),
        ]
        extra = dict(collective_id=0, has_side_effects=True)
    return pl.pallas_call(
        functools.partial(interact_body, layers, HEADS, firsts, slots, fld, rep),
        out_shape=(jax.ShapeDtypeStruct(out_shape, bf16), jax.ShapeDtypeStruct((1, lanes), f32)),
        in_specs=[pl.BlockSpec(memory_space=pltpu.VMEM)] * 3,
        out_specs=(pl.BlockSpec(memory_space=pltpu.VMEM),) * 2,
        scratch_shapes=[
            pltpu.VMEM((fields, width, lanes), bf16), flat, flat, flat, flat, flat,
            pltpu.VMEM((fields, fields, lanes), f32), flat,
        ] + links,
        compiler_params=pltpu.CompilerParams(vmem_limit_bytes=40 << 20, **extra),
    )(found, wt, ow)


def lookup_body(ready, starts, shifts, valid, table, out, held, sems):
    tiles, slots, width, lanes = out.shape
    piece = table.shape[1] // sems.shape[0]
    copies = [
        pltpu.make_async_copy(
            table.at[:, c * piece:(c + 1) * piece], held.at[:, c * piece:(c + 1) * piece], sems.at[c]
        )
        for c in range(sems.shape[0])
    ]
    for copy in copies:
        copy.start()
    lane = lax.broadcasted_iota(jnp.int32, (1, lanes), 1)
    done = 0
    for j in range(slots):
        while done < len(copies) and done * piece < ready[j]:
            copies[done].wait()
            done += 1

        def tile(t, carry):
            base = (j * tiles + t) * lanes
            acc = jnp.zeros((width, lanes), bf16)
            for i in range(lanes):
                start = pl.multiple_of(starts[base + i], 128)
                block = pltpu.roll(held[:, pl.ds(start, lanes)], shifts[base + i], 1)
                acc = jnp.where(lane == i, block, acc)
            keep = valid[j, pl.ds(t, 1), :] > 0
            out[t, j] = jnp.where(keep, acc, jnp.zeros_like(acc))
            return carry
        lax.fori_loop(0, tiles, tile, 0)
    for copy in copies[done:]:
        copy.wait()


def pieces(owned):
    return next(c for c in (5, 4, 3, 2, 1) if owned % (c * 128) == 0)


def lookup(starts, shifts, valid, table_t, ready):
    slots, tiles, lanes = valid.shape
    width, owned = table_t.shape
    return pl.pallas_call(
        functools.partial(lookup_body, ready),
        out_shape=jax.ShapeDtypeStruct((tiles, slots, width, lanes), bf16),
        in_specs=[
            pl.BlockSpec(memory_space=pltpu.SMEM),
            pl.BlockSpec(memory_space=pltpu.SMEM),
            pl.BlockSpec(memory_space=pltpu.VMEM),
            pl.BlockSpec(memory_space=pl.ANY),
        ],
        out_specs=pl.BlockSpec(memory_space=pltpu.VMEM),
        scratch_shapes=[
            pltpu.VMEM((width, owned), bf16),
            pltpu.SemaphoreType.DMA((pieces(owned),)),
        ],
        compiler_params=pltpu.CompilerParams(vmem_limit_bytes=48 << 20),
    )(starts, shifts, valid, table_t)


def per_device(
    feature_ids, field_slot, table, query_weight, key_weight, value_weight, residual_weight, out_weight
):
    examples, slots = feature_ids.shape
    owned, width = table.shape
    fld = lax.axis_size("fld")
    rep = lax.axis_size("rep")
    me = lax.axis_index("rep")
    rows_slot = owned * rep // slots
    lanes = examples // rep // fld
    firsts = [r * owned // rows_slot for r in range(rep)]
    lasts = [-(-(r + 1) * owned // rows_slot) for r in range(rep)]
    near = max(b - a for a, b in zip(firsts, lasts))
    firsts = [min(a, slots - near) for a in firsts]
    ready = [
        max(min(owned, (a + j + 1) * rows_slot - r * owned) for r, a in enumerate(firsts))
        for j in range(near)
    ]
    first = sum((me == r) * a for r, a in enumerate(firsts)).astype(jnp.int32)
    near_ids = lax.dynamic_slice_in_dim(jnp.transpose(feature_ids), first, near, 0)
    offset = (first + jnp.arange(near, dtype=jnp.int32)) * rows_slot - me * owned
    rows = near_ids + offset[:, None]
    valid = ((rows >= 0) & (rows < owned)).astype(jnp.int32)
    rows = jnp.clip(rows, 0, owned - 1)
    starts = (rows >> 7) << 7
    shifts = (jnp.arange(examples, dtype=jnp.int32)[None, :] - rows) & 127
    found = lookup(
        starts.reshape(-1), shifts.reshape(-1), valid.reshape(near, -1, lanes), jnp.transpose(table), ready
    )
    joined = jnp.concatenate([query_weight, key_weight, value_weight, residual_weight], axis=2)
    weights = jnp.swapaxes(joined, 1, 2)
    fields = field_slot.shape[0]
    if fields == fld * slots:
        order = field_slot[:, None] == jnp.arange(fields, dtype=jnp.int32)[None, :]
        weight_t = jnp.sum(jnp.where(order[:, None, :], out_weight[:, :, None], 0.0), axis=0)
        back, logits = interact(found, weights, weight_t, firsts, slots, fld, rep)
        return jnp.swapaxes(back, 1, 2), logits
    found = found.reshape(rep, fld, near, width, lanes)
    looked = jnp.zeros((fld, slots, width, lanes), bf16)
    looked = lax.dynamic_update_slice_in_dim(looked, lax.dynamic_index_in_dim(found, me, 0, False), first, 1)
    for step in range(1, rep):
        route = [(r, (r + step) % rep) for r in range(rep)]
        other = lax.ppermute(lax.dynamic_index_in_dim(found, (me + step) % rep, 0, False), "rep", route)
        source = (me - step) % rep
        start = sum((source == r) * a for r, a in enumerate(firsts)).astype(jnp.int32)
        old = lax.dynamic_slice_in_dim(looked, start, near, 1)
        looked = lax.dynamic_update_slice_in_dim(looked, old + other, start, 1)
    arrived = lax.all_to_all(looked, "fld", split_axis=0, concat_axis=0, tiled=True)
    layer_in = jnp.take(arrived.reshape(fld * slots, width, lanes), field_slot, axis=0)
    weight_t = jnp.transpose(out_weight)
    hidden, logits = interact(layer_in[:, None], weights, weight_t, [0], 1, 0, 0)
    hidden = jnp.zeros((fld * slots, width, lanes), bf16).at[field_slot].set(hidden)
    placed = hidden.reshape(fld, slots, width, lanes)
    back = lax.all_to_all(placed, "fld", split_axis=0, concat_axis=0, tiled=True)
    interacted = jnp.transpose(back, (1, 0, 3, 2)).reshape(slots, fld * lanes, width)
    return interacted, logits


def solution(mesh):
    placed = (P("groups", "fld"), P(), P(("fld", "rep"), None), P(), P(), P(), P(), P())
    return jax.shard_map(
        per_device,
        mesh=mesh,
        in_specs=placed,
        out_specs=(P("fld", ("groups", "rep"), None), P("rep", ("groups", "fld"))),
        check_vma=False,
    )
```

time: 119 us -> 103 us (0.87)
  Pallas kernels: 64.6 us -> 92.5 us
  blocking collectives: 21.2 us -> 0 us
  waiting for transfers between devices: 17 us -> 0 us
  starting transfers between devices: 7.33 us -> 0 us
  local copies, waits for them, and re-layouts: 3.27 us -> 4.88 us
    pallas_call x1, Pallas kernels: 25.5 us -> 54.3 us  [interact(): pl.pallas_call(functools.partial(interact_body, layers, HEADS, firsts, sl...]
    all_to_all x1 -> x0, blocking collectives: 21.2 us -> none  [per_device(): lax.all_to_all(placed, 'fld', split_axis=0, concat_axis=0, tiled=True)]
    all_to_all x1 -> x0, waiting for transfers between devices: 17 us -> none  [per_device(): lax.all_to_all(looked, 'fld', split_axis=0, concat_axis=0, tiled=True)]
    all_to_all x1 -> x0, starting transfers between devices: 6.97 us -> none  [per_device(): lax.all_to_all(looked, 'fld', split_axis=0, concat_axis=0, tiled=True)]
    unnamed x17 -> x7, local copies, waits for them, and re-layouts: 0.41 us -> 4.77 us
    dynamic_update_slice x1 -> x0, other arithmetic: 1.87 us -> none  [per_device(): looked = lax.dynamic_update_slice_in_dim(looked, old + got, start, 1)]
  transfers between devices with their start and end apart: 2 -> 0, of which waited for: 1 -> 0; matrix products, arithmetic and copies ran while one was open for 2% -> 0% of each run, Pallas kernels for 0% -> 0%
where the time goes in v2:
time: 103 us; the launch traced here: 102 us
  Pallas kernels  92.5 us (90%)
  local copies, waits for them, and re-layouts  4.88 us (5%)
  other arithmetic  3.64 us (4%)
    pallas_call x1, Pallas kernels, interact(): pl.pallas_call(functools.partial(interact_body, layers, HEADS, firsts, sl...  54.3 us
    pallas_call x1, Pallas kernels, lookup(): pl.pallas_call(functools.partial(lookup_body, ready), out_shape=jax.Shape...  38.2 us
    unnamed x7, local copies, waits for them, and re-layouts  4.77 us

profile of v2, /device:TPU:0, one launch (start us, length us, event | category | flops | bytes accessed | tf_op | source)
XLA Modules:
  0.0 101.7 jit_solution(11879960449015346153)
XLA Ops:
  0.6 0.7 iota_compare_fusion
  1.4 1.0 select_reduce_fusion
  2.4 0.1 copy.18.ow
  2.5 0.9 copy.14
  3.3 0.9 copy.15
  4.2 0.9 copy.16
  5.0 0.9 copy.17
  5.9 0.9 convert_bitcast_fusion
  6.9 0.9 fusion.1
  7.9 38.2 %shard_map.95.found = bf16[16,3,64,128]{3,2,1,0:T(8,128)(2,1)S(1)} custom-call(s32[6144]{0:T(1024)S(1)} %reshape.39.starts, s32[6144]{0:T(1024)S(1)} %reshape.40.shifts, s32[3,16,128]{2,1,0:T(8,128)S(1)} %bitcast.18, bf16[64,163840]{1,0:T(8,128)(2,1)} %bitcast.19), custom_call_target="tpu_custom_call" | custom-call | tf_op jit(solution)/shard_map/pallas_call | solution.py:264
  46.0 54.3 %shard_map.96 = (bf16[5,64,1024]{2,1,0:T(8,128)(2,1)S(1)}, f32[1,128]{1,0:T(1,128)S(1)}) custom-call(bf16[16,3,64,128]{3,2,1,0:T(8,128)(2,1)S(1)} %shard_map.95.found, bf16[2,256,64]{2,1,0:T(8,128)(2,1)S(1)} %maximum_bitcast_fusion.wt, f32[64,40]{1,0:T(8,128)S(1)} %copy.18.ow), custom_call_target="tpu_custom_call" | custom-call | tf_op jit(solution)/shard_map/pallas_call | solution.py:211
  100.4 0.8 copy.24
  101.2 0.5 copy.25
  (5 shorter events, 0.1 us)

commit v3 on v2

--- a/solution.py
+++ b/solution.py
@@ -22,8 +22,8 @@
 
 
 def interact_body(
-    layers, heads, firsts, slots, fld, rep, found, wt, ow, out, logit,
-    xs, q, k, v, skip, qt, att, mt, *links
+    layers, heads, firsts, slots, fld, rep, found, wq, wk, wv, ws, ow, out, logit,
+    wt, xs, q, k, v, skip, qt, att, mt, *links
 ):
     fields, width, lanes = xs.shape
     near = found.shape[1]
@@ -62,6 +62,10 @@
                 send_sem=send.at[h, n], recv_sem=recv.at[h, n],
                 device_id={"fld": dest}, device_id_type=MESH,
             )
+
+    for l in range(layers):
+        for n, w in enumerate((wq, wk, wv, ws)):
+            wt[l, n * width:(n + 1) * width, :] = jnp.transpose(w[l].astype(f32)).astype(bf16)
 
     def project_one(l, f, value):
         p = jnp.dot(wt[l], value, preferred_element_type=f32)
@@ -189,10 +193,10 @@
             hop(n, c).wait_send()
 
 
-def interact(found, wt, ow, firsts, slots, fld, rep):
+def interact(found, weights, ow, firsts, slots, fld, rep):
     fields = ow.shape[1]
     near, width, lanes = found.shape[1:]
-    layers = wt.shape[0]
+    layers = weights[0].shape[0]
     flat = pltpu.VMEM((fields * width, lanes), f32)
     out_shape, links, extra = (fields, width, lanes), [], {}
     if fld:
@@ -211,14 +215,15 @@
     return pl.pallas_call(
         functools.partial(interact_body, layers, HEADS, firsts, slots, fld, rep),
         out_shape=(jax.ShapeDtypeStruct(out_shape, bf16), jax.ShapeDtypeStruct((1, lanes), f32)),
-        in_specs=[pl.BlockSpec(memory_space=pltpu.VMEM)] * 3,
+        in_specs=[pl.BlockSpec(memory_space=pltpu.VMEM)] * 6,
         out_specs=(pl.BlockSpec(memory_space=pltpu.VMEM),) * 2,
         scratch_shapes=[
+            pltpu.VMEM((layers, 4 * width, width), bf16),
             pltpu.VMEM((fields, width, lanes), bf16), flat, flat, flat, flat, flat,
             pltpu.VMEM((fields, fields, lanes), f32), flat,
         ] + links,
         compiler_params=pltpu.CompilerParams(vmem_limit_bytes=40 << 20, **extra),
-    )(found, wt, ow)
+    )(found, *weights, ow)
 
 
 def lookup_body(ready, starts, shifts, valid, table, out, held, sems):
@@ -308,8 +313,7 @@
     found = lookup(
         starts.reshape(-1), shifts.reshape(-1), valid.reshape(near, -1, lanes), jnp.transpose(table), ready
     )
-    joined = jnp.concatenate([query_weight, key_weight, value_weight, residual_weight], axis=2)
-    weights = jnp.swapaxes(joined, 1, 2)
+    weights = (query_weight, key_weight, value_weight, residual_weight)
     fields = field_slot.shape[0]
     if fields == fld * slots:
         order = field_slot[:, None] == jnp.arange(fields, dtype=jnp.int32)[None, :]

time: 103 us -> 99.7 us (0.968)
  local copies, waits for them, and re-layouts: 4.88 us -> 1.49 us
    unnamed x7 -> x11, local copies, waits for them, and re-layouts: 4.77 us -> 1.37 us
where the time goes in v3:
time: 99.7 us; the launch traced here: 98.3 us
  Pallas kernels  92.5 us (93%)
  other arithmetic  3.61 us (4%)
  local copies, waits for them, and re-layouts  1.49 us (1%)
    pallas_call x1, Pallas kernels, interact(): pl.pallas_call(functools.partial(interact_body, layers, HEADS, firsts, sl...  54.3 us
    pallas_call x1, Pallas kernels, lookup(): pl.pallas_call(functools.partial(lookup_body, ready), out_shape=jax.Shape...  38.2 us

profile of v3, /device:TPU:0, one launch (start us, length us, event | category | flops | bytes accessed | tf_op | source)
XLA Modules:
  0.0 98.3 jit_solution(212426286548131381)
XLA Ops:
  0.6 0.0 copy-start.3
  0.6 0.0 copy-start.2
  0.7 0.0 copy-start.1
  0.7 0.0 copy-start
  0.7 0.7 iota_compare_fusion
  1.4 1.0 %select_reduce_fusion = f32[64,40]{0,1:T(8,128)S(1)} fusion(f32[40,64]{1,0:T(8,128)} %param.15, pred[40,40]{1,0:T(8,128)(4,1)S(1)} %iota_compare_fusion), kind=kLoop, calls=%fused_computation | loop fusion | flops 202240 | bytes 22080 | tf_op jit(solution)/shard_map/reduce_sum | solution.py:320
  2.4 0.1 copy.10.ow
  2.5 0.9 convert_bitcast_fusion
  3.5 0.9 fusion.1
  4.5 38.2 %shard_map.95.found = bf16[16,3,64,128]{3,2,1,0:T(8,128)(2,1)S(1)} custom-call(s32[6144]{0:T(1024)S(1)} %reshape.39.starts, s32[6144]{0:T(1024)S(1)} %reshape.40.shifts, s32[3,16,128]{2,1,0:T(8,128)S(1)} %bitcast.16, bf16[64,163840]{1,0:T(8,128)(2,1)} %bitcast.17), custom_call_target="tpu_custom_call" | custom-call | tf_op jit(solution)/shard_map/pallas_call | solution.py:269
  42.6 0.0 copy-done.3
  42.6 0.0 copy-done.2
  42.6 0.0 copy-done.1
  42.7 0.0 copy-done
  42.7 54.3 %shard_map.96 = (bf16[5,64,1024]{2,1,0:T(8,128)(2,1)S(1)}, f32[1,128]{1,0:T(1,128)S(1)}) custom-call(bf16[16,3,64,128]{3,2,1,0:T(8,128)(2,1)S(1)} %shard_map.95.found, bf16[2,64,64]{2,1,0:T(8,128)(2,1)S(1)} %copy-done, bf16[2,64,64]{2,1,0:T(8,128)(2,1)S(1)} %copy-done.1, bf16[2,64,64]{2,1,0:T(8,128)(2,1)S(1)} %copy-done.2, bf16[2,64,64]{2,1,0:T(8,128)(2,1)S(1)} %copy-done.3, ...), custom_call_target="tpu_custom_call" | custom-call | tf_op jit(solution)/shard_map/pallas_call | solution.py:215
  97.0 0.8 copy.16
  97.8 0.5 copy.17
  (4 shorter events, 0.0 us)
Async XLA Ops:
  0.6 42.0 %copy-start.3 = (bf16[2,64,64]{2,1,0:T(8,128)(2,1)S(1)}, bf16[2,64,64]{2,1,0:T(8,128)(2,1)}, u32[]{:S(2)}) copy-start(bf16[2,64,64]{2,1,0:T(8,128)(2,1)} %ws.1) | copy-start | bytes 49156
  0.6 42.0 %copy-start.2 = (bf16[2,64,64]{2,1,0:T(8,128)(2,1)S(1)}, bf16[2,64,64]{2,1,0:T(8,128)(2,1)}, u32[]{:S(2)}) copy-start(bf16[2,64,64]{2,1,0:T(8,128)(2,1)} %wv.1) | copy-start | bytes 49156
  0.7 42.0 %copy-start.1 = (bf16[2,64,64]{2,1,0:T(8,128)(2,1)S(1)}, bf16[2,64,64]{2,1,0:T(8,128)(2,1)}, u32[]{:S(2)}) copy-start(bf16[2,64,64]{2,1,0:T(8,128)(2,1)} %wk.1) | copy-start | bytes 49156
  0.7 42.0 %copy-start = (bf16[2,64,64]{2,1,0:T(8,128)(2,1)S(1)}, bf16[2,64,64]{2,1,0:T(8,128)(2,1)}, u32[]{:S(2)}) copy-start(bf16[2,64,64]{2,1,0:T(8,128)(2,1)} %wq.1) | copy-start | bytes 49156
